TPU v7x, 512 devices: a whole 4x4x16 slice. The times are simulated.
512 devices in a mesh: segment: 8 (over z_lo), seq: 16 (over z_hi, y, core), head: 4 (over x).
Axes of the slice: x: 4, y: 4, z: 16 (z_hi: 2, z_lo: 8; z = z_hi * 8 + z_lo), core: 2. Of those that a mesh axis runs over, the one named last changes fastest.
Arguments:
- tokens: bfloat16 [8, 4096, 1536], P('segment', ('seq', 'head'))
- lengths: int32 [8], replicated, may hold values from 2048 to 4096, as said below
- modulation: bfloat16 [8, 2, 1536], P('segment'), may hold values from -0.5 to 0.5
- gate_gain: bfloat16 [8, 1536], P('segment'), may hold values from 1 to 3
- w_qkv: bfloat16 [8, 1536, 3, 1536], P('segment', None, None, 'head')
- w_out: bfloat16 [8, 1536, 1536], P('segment', 'head'), may hold values from -0.15625 to 0.15625
Outputs:
- states: bfloat16 [8, 4096, 1536], P('segment', ('seq', 'head'))
Inputs may be any that keep to these rules, and one draw needn't show every extreme that they name: Micro-batch m has lengths[m] real tokens at the start of its 4096 slots; some micro-batch fills all 4096.
All inputs are finite; a program needn't handle non-finite values.
Results may differ from a plain program's by a relative error of at most 0.02.
Values may be sent and summed in bfloat16 or wider, within the bound.
A program may use at most 64 MiB of HBM per device.

v0:
```python
import jax
import jax.numpy as jnp
from jax import lax
from jax.sharding import PartitionSpec as P

HEAD = 128
TICKS = 2


def from_behind(value, axis, by):
    length = lax.axis_size(axis)
    return lax.ppermute(value, axis, [(i, (i + by) % length) for i in range(length)])


def layer_norm(values):
    row_mean = jnp.mean(values, axis=-1, keepdims=True)
    centered = values - row_mean
    row_var = jnp.mean(centered * centered, axis=-1, keepdims=True)
    return centered / jnp.sqrt(row_var + 1e-06)


def block_size(key_count, shard_rows):
    for candidate in (1024, 512):
        return candidate
    if key_count <= 1024:
        return key_count
    return shard_rows


def attend_block(running, query_heads, key_block, value_block, first_row, length, score_scale):
    row_max, row_sum, weighted = running
    key_count = key_block.shape[0]
    local_heads = query_heads.shape[1]
    head_size = query_heads.shape[2]
    key_heads = key_block.reshape(key_count, local_heads, head_size)
    value_heads = value_block.reshape(key_count, local_heads, head_size)
    scores = (
        jnp.einsum("rhd,khd->hrk", query_heads, key_heads, preferred_element_type=jnp.float32)
        * score_scale
    )
    key_valid = first_row + jnp.arange(key_count, dtype=jnp.int32) < length
    scores = jnp.where(key_valid[None, None, :], scores, -1e30)
    new_max = jnp.maximum(row_max, jnp.max(scores, axis=2))
    exponent = jnp.where(key_valid[None, None, :], jnp.exp(scores - new_max[:, :, None]), 0.0)
    rescale = jnp.exp(row_max - new_max)
    row_sum = row_sum * rescale + jnp.sum(exponent, axis=2)
    weighted = weighted * rescale[:, :, None] + jnp.einsum(
        "hrk,khd->hrd",
        exponent.astype(jnp.bfloat16),
        value_heads,
        preferred_element_type=jnp.float32,
    )
    return (new_max, row_sum, weighted)


def attend_piece(running, pieces, query_heads, length, score_scale, shard_rows):
    key_piece, value_piece = pieces
    key_count = key_piece.shape[0]
    block = block_size(key_count, shard_rows)
    blocks = key_count // block
    key_stack = key_piece.reshape(blocks, block, key_piece.shape[1])
    value_stack = value_piece.reshape(blocks, block, value_piece.shape[1])

    def step_block(state_now, inputs):
        key_block, value_block, block_index = inputs
        return (
            attend_block(
                state_now,
                query_heads,
                key_block,
                value_block,
                block_index * block,
                length,
                score_scale,
            ),
            None,
        )

    final, unused = lax.scan(
        step_block, running, (key_stack, value_stack, jnp.arange(blocks, dtype=jnp.int32))
    )
    return final


def per_device(tokens, lengths, modulation, gate_gain, w_qkv, w_out):
    segment_count = lax.axis_size("segment")
    position = lax.axis_index("segment")
    state = tokens[0]
    shift_scale = modulation[0].astype(jnp.float32)
    gate_row = gate_gain[0].astype(jnp.float32)
    model_width = w_qkv.shape[1]
    local_width = w_qkv.shape[3]
    local_heads = local_width // HEAD
    flat_qkv = w_qkv[0].reshape(model_width, 3 * local_width)
    out_heads = w_out[0].reshape(local_heads, HEAD, model_width)
    score_scale = HEAD ** (-0.5)
    for tick_index in range(TICKS):
        micro_index = (position - tick_index) % segment_count
        length = lax.dynamic_index_in_dim(lengths, micro_index, 0, keepdims=False)
        values = state.astype(jnp.float32)
        normed = (layer_norm(values) * (1.0 + shift_scale[1]) + shift_scale[0]).astype(jnp.bfloat16)
        projected = jnp.dot(
            lax.all_gather(normed, "head", axis=0, tiled=True),
            flat_qkv,
            preferred_element_type=jnp.float32,
        ).astype(jnp.bfloat16)
        query_rows = projected.shape[0]
        query_heads = projected[:, :local_width].reshape(query_rows, local_heads, HEAD)
        key_part = projected[:, local_width : 2 * local_width]
        value_part = projected[:, 2 * local_width :]
        initial = (
            jnp.full((local_heads, query_rows), -1e30, jnp.float32),
            jnp.zeros((local_heads, query_rows), jnp.float32),
            jnp.zeros((local_heads, query_rows, HEAD), jnp.float32),
        )
        running = attend_piece(
            initial,
            (
                lax.all_gather(key_part, "seq", axis=0, tiled=True),
                lax.all_gather(value_part, "seq", axis=0, tiled=True),
            ),
            query_heads,
            length,
            score_scale,
            query_rows,
        )
        attended = (running[2] / running[1][:, :, None]).astype(jnp.bfloat16)
        branch = lax.psum_scatter(
            jnp.einsum(
                "hrd,hdn->rn", attended, out_heads, preferred_element_type=jnp.float32
            ).astype(jnp.bfloat16),
            "head",
            scatter_dimension=0,
            tiled=True,
        ).astype(jnp.float32)
        updated = (values + gate_row * branch).astype(jnp.bfloat16)
        state = from_behind(updated, "segment", 1)
    return state[None]


def solution(mesh):
    return jax.shard_map(
        per_device,
        mesh=mesh,
        in_specs=(
            P("segment", ("seq", "head"), None),
            P(),
            P("segment", None, None),
            P("segment", None),
            P("segment", None, None, "head"),
            P("segment", "head", None),
        ),
        out_specs=P("segment", ("seq", "head"), None),
        check_vma=False,
    )
```

profile of v0, /device:TPU:8, one launch (start us, length us, event | category | flops | bytes accessed | tf_op | source)
XLA Modules:
  0.0 673.3 jit_solution(7717919724192401937)
XLA Ops:
  6.5 0.8 convert_element_type.59
  7.4 1.1 convert_reduce_fusion.1
  8.5 1.2 fusion.42
  9.6 1.1 fusion.45
  10.7 13.7 %all_gather.18 = bf16[256,1536]{1,0:T(8,128)(2,1)S(1)} all-gather(bf16[64,1536]{1,0:T(8,128)(2,1)S(1)} %fusion.45), channel_id=1, replica_groups=mesh['segment'=8,'seq'=16,'head'=4] {'head'}, dimensions={0}, use_global_device_ids=true | all-gather | bytes 983040 | tf_op jit(solution)/shard_map/all_gather | solution.py:103
  24.4 6.1 copy.17
  30.5 3.2 convolution_convert_fusion.1
  33.7 0.8 fusion.52
  35.6 0.8 copy.20
  37.0 108.7 %all-gather.5.cloned.1.call-done = bf16[4096,384]{1,0:T(8,128)(2,1)} async-done(((bf16[256,384]{1,0:T(8,128)(2,1)}), bf16[4096,384]{1,0:T(8,128)(2,1)}) %all-gather.5.cloned.1.call-update) | async-done | bytes 3145744 | tf_op jit(solution)/shard_map/all_gather | solution.py:119
  145.6 101.3 %all-gather.7.cloned.1.call-done = bf16[4096,384]{1,0:T(8,128)(2,1)} async-done(((bf16[256,384]{1,0:T(8,128)(2,1)}), bf16[4096,384]{1,0:T(8,128)(2,1)}) %all-gather.7.cloned.1.call-update) | async-done | bytes 3145744 | tf_op jit(solution)/shard_map/all_gather | solution.py:120
  246.9 56.6 %while.30 = (s32[]{:T(128)}, f32[3,256]{1,0:T(4,128)S(1)}, f32[3,256]{1,0:T(4,128)S(1)}, f32[3,256,128]{2,1,0:T(8,128)}, s32[4]{0:T(128)S(1)}, /*index=5*/s32[]{...) while((s32[]{:T(128)}, f32[3,256]{1,0:T(4,128)S(1)}, ...), condition=%wide.region_5.6_spmd.clone, body=%wide.region_2.5_spmd.clone.sunk | while | flops 413177600 | bytes 21483740 | solution.py:79
  248.8 1.5 constant_dynamic-slice_fusion.6
  250.6 3.4 bitcast_reduce_fusion.4
  254.0 2.5 fusion.84
  256.9 3.4 fusion.86
  260.3 0.8 copy-done.13
  262.9 1.5 constant_dynamic-slice_fusion.6
  264.7 3.4 bitcast_reduce_fusion.4
  268.2 2.5 fusion.84
  271.0 3.4 fusion.86
  274.5 0.8 copy-done.13
  277.1 1.5 constant_dynamic-slice_fusion.6
  278.9 3.4 bitcast_reduce_fusion.4
  282.3 2.5 fusion.84
  285.2 3.4 fusion.86
  291.2 1.5 constant_dynamic-slice_fusion.6
  293.0 3.4 bitcast_reduce_fusion.4
  296.5 2.5 fusion.84
  299.3 3.4 fusion.86
  302.8 0.8 copy-done.13
  303.6 2.6 fusion.30
  306.2 21.7 %reduce-scatter.3.cloned.1.call-done = bf16[64,1536]{1,0:T(8,128)(2,1)} async-done(((bf16[256,1536]{1,0:T(8,128)(2,1)}), bf16[64,1536]{1,0:T(8,128)(2,1)}) %reduce-scatter.3.cloned.1.call-update) | async-done | bytes 196624 | tf_op jit(solution)/shard_map/reduce_scatter | solution.py:128
  328.0 1.0 fusion.46
  329.0 3.5 collective-permute-start
  332.4 11.0 %collective-permute-done = bf16[64,1536]{1,0:T(8,128)(2,1)S(1)} collective-permute-done((bf16[64,1536]{1,0:T(8,128)(2,1)S(1)}, bf16[64,1536]{1,0:T(8,128)(2,1)S(1)}, u32[]{:S(2)}, u32[]{:S(2)}) %collective-permute-start) | collective-permute-done | bytes 196640 | tf_op jit(solution)/shard_map/ppermute | solution.py:12
  344.2 13.6 %all_gather.21 = bf16[256,1536]{1,0:T(8,128)(2,1)S(1)} all-gather(bf16[64,1536]{1,0:T(8,128)(2,1)S(1)} %fusion.41), channel_id=1, replica_groups=mesh['segment'=8,'seq'=16,'head'=4] {'head'}, dimensions={0}, use_global_device_ids=true | all-gather | bytes 983040 | tf_op jit(solution)/shard_map/all_gather | solution.py:103
  357.9 3.2 convolution_convert_fusion
  361.1 0.8 fusion.51
  362.8 0.8 copy.24
  363.6 104.3 %all-gather.11.cloned.1.call-done = bf16[4096,384]{1,0:T(8,128)(2,1)} async-done(((bf16[256,384]{1,0:T(8,128)(2,1)}), bf16[4096,384]{1,0:T(8,128)(2,1)}) %all-gather.11.cloned.1.call-update) | async-done | bytes 3145744 | tf_op jit(solution)/shard_map/all_gather | solution.py:120
  467.9 101.2 %all-gather.9.cloned.1.call-done = bf16[4096,384]{1,0:T(8,128)(2,1)} async-done(((bf16[256,384]{1,0:T(8,128)(2,1)}), bf16[4096,384]{1,0:T(8,128)(2,1)}) %all-gather.9.cloned.1.call-update) | async-done | bytes 3145744 | tf_op jit(solution)/shard_map/all_gather | solution.py:119
  569.1 56.8 %while.31 = (s32[]{:T(128)}, f32[3,256]{1,0:T(4,128)S(1)}, f32[3,256]{1,0:T(4,128)S(1)}, f32[3,256,128]{2,1,0:T(8,128)}, s32[4]{0:T(128)S(1)}, /*index=5*/s32[]{...) while((s32[]{:T(128)}, f32[3,256]{1,0:T(4,128)S(1)}, ...), condition=%wide.region_12.13_spmd.clone, body=%wide.region_9.12_spmd.clone.sunk | while | flops 413177600 | bytes 21483740 | solution.py:79
  571.0 1.5 constant_dynamic-slice_fusion.7
  572.8 3.5 bitcast_reduce_fusion.5
  576.3 2.5 fusion.91
  579.1 3.4 fusion.93
  585.2 1.5 constant_dynamic-slice_fusion.7
  587.0 3.5 bitcast_reduce_fusion.5
  590.5 2.5 fusion.91
  593.3 3.4 fusion.93
  599.4 1.5 constant_dynamic-slice_fusion.7
  601.2 3.5 bitcast_reduce_fusion.5
  604.7 2.5 fusion.91
  607.5 3.4 fusion.93
  613.6 1.5 constant_dynamic-slice_fusion.7
  615.4 3.5 bitcast_reduce_fusion.5
  618.9 2.5 fusion.91
  621.7 3.4 fusion.93
  625.9 2.6 fusion.31
  628.5 21.8 %reduce-scatter.5.cloned.1.call-done = bf16[64,1536]{1,0:T(8,128)(2,1)} async-done(((bf16[256,1536]{1,0:T(8,128)(2,1)}), bf16[64,1536]{1,0:T(8,128)(2,1)}) %reduce-scatter.5.cloned.1.call-update) | async-done | bytes 196624 | tf_op jit(solution)/shard_map/reduce_scatter | solution.py:128
  650.3 1.0 fusion.47
  651.3 3.5 collective-permute-start.1
  654.8 11.0 %collective-permute-done.1 = bf16[64,1536]{1,0:T(8,128)(2,1)S(1)} collective-permute-done((bf16[64,1536]{1,0:T(8,128)(2,1)S(1)}, bf16[64,1536]{1,0:T(8,128)(2,1)S(1)}, u32[]{:S(2)}, u32[]{:S(2)}) %collective-permute-start.1) | collective-permute-done | bytes 196640 | tf_op jit(solution)/shard_map/ppermute | solution.py:12
  (142 shorter events, 22.2 us)
Async XLA Ops:
  6.5 297.0 %copy-start = (bf16[1,384,1536]{2,1,0:T(8,128)(2,1)S(1)}, bf16[1,384,1536]{2,1,0:T(8,128)(2,1)}, u32[]{:S(2)}) copy-start(bf16[1,384,1536]{2,1,0:T(8,128)(2,1)} %param.15) | copy-start | bytes 3538948
  6.5 139.1 %all-gather.5.cloned.1.call-start = ((), (), s32[]{:S(2)}) async-start(), calls=%async_computation.2 | async-start | bytes 3342336 | tf_op jit(solution)/shard_map/all_gather | solution.py:119
  7.4 2.3 copy-start.6
  7.4 3.3 copy-start.8
  30.5 5.9 copy-start.11
  34.5 212.4 %all-gather.7.cloned.1.call-start = ((), (), s32[]{:S(2)}) async-start(), calls=%async_computation.3 | async-start | bytes 3342336 | tf_op jit(solution)/shard_map/all_gather | solution.py:120
  35.3 292.7 %reduce-scatter.3.cloned.1.call-start = ((), (), s32[]{:S(2)}) async-start(), calls=%async_computation.4 | async-start | bytes 983040 | tf_op jit(solution)/shard_map/reduce_scatter | solution.py:128
  254.0 2.8 copy-start.12
  260.3 0.8 copy-start.13
  268.2 2.8 copy-start.12
  274.4 0.8 copy-start.13
  282.3 2.8 copy-start.12
  288.6 0.8 copy-start.13
  296.5 2.8 copy-start.12
  302.7 0.8 copy-start.13
  303.5 2.7 copy-start.10
  303.5 24.4 %copy-start.1 = (bf16[1,64,1536]{2,1,0:T(8,128)(2,1)S(1)}, bf16[1,64,1536]{2,1,0:T(8,128)(2,1)}, u32[]{:S(2)}) copy-start(bf16[1,64,1536]{2,1,0:T(8,128)(2,1)} %param.10) | copy-start | bytes 589828
  303.5 40.5 %copy-start.7 = (f32[1536]{0:T(1024)S(1)}, f32[1536]{0:T(1024)}, u32[]{:S(2)}) copy-start(f32[1536]{0:T(1024)} %copy-done.6) | copy-start | bytes 18436
  303.5 40.5 %copy-start.9 = (f32[1536]{0:T(1024)S(1)}, f32[1536]{0:T(1024)}, u32[]{:S(2)}) copy-start(f32[1536]{0:T(1024)} %copy-done.8) | copy-start | bytes 18436
  306.1 161.8 %all-gather.11.cloned.1.call-start = ((), (), s32[]{:S(2)}) async-start(), calls=%async_computation.6 | async-start | bytes 3342336 | tf_op jit(solution)/shard_map/all_gather | solution.py:120
  306.2 54.9 %copy-start.4 = (f32[1536]{0:T(1024)}, f32[1536]{0:T(1024)S(1)}, u32[]{:S(2)}) copy-start(f32[1536]{0:T(1024)S(1)} %convert_reduce_fusion.2) | copy-start | bytes 18436
  329.0 14.4 %collective-permute-start = (bf16[64,1536]{1,0:T(8,128)(2,1)S(1)}, bf16[64,1536]{1,0:T(8,128)(2,1)S(1)}, u32[]{:S(2)}, u32[]{:S(2)}) collective-permute-start(bf16[64,1536]{1,0:T(8,128)(2,1)S(1)} %fusion.46), channel_id=1, source_target_pairs={{0,64},{64,128},{128,192},{192,256},{256,320},{320,384},{384,448},... | collective-permute-start | bytes 589832 | tf_op jit(solution)/shard_map/ppermute | solution.py:12
  343.4 0.7 copy-start.2
  362.0 207.1 %all-gather.9.cloned.1.call-start = ((), (), s32[]{:S(2)}) async-start(), calls=%async_computation.5 | async-start | bytes 3342336 | tf_op jit(solution)/shard_map/all_gather | solution.py:119
  362.6 287.7 %reduce-scatter.5.cloned.1.call-start = ((), (), s32[]{:S(2)}) async-start(), calls=%async_computation.7 | async-start | bytes 983040 | tf_op jit(solution)/shard_map/reduce_scatter | solution.py:128
  576.3 2.8 copy-start.14
  582.6 0.7 copy-start.15
  590.5 2.8 copy-start.14
  596.8 0.7 copy-start.15
  604.7 2.8 copy-start.14
  611.0 0.7 copy-start.15
  618.9 2.8 copy-start.14
  625.2 0.7 copy-start.15
  625.9 24.4 %copy-start.3 = (bf16[64,1536]{1,0:T(8,128)(2,1)S(1)}, bf16[64,1536]{1,0:T(8,128)(2,1)}, u32[]{:S(2)}) copy-start(bf16[64,1536]{1,0:T(8,128)(2,1)} %copy-done.2) | copy-start | bytes 589828
  625.9 24.4 %copy-start.5 = (f32[1536]{0:T(1024)S(1)}, f32[1536]{0:T(1024)}, u32[]{:S(2)}) copy-start(f32[1536]{0:T(1024)} %copy-done.4) | copy-start | bytes 18436
  651.3 14.5 %collective-permute-start.1 = (bf16[64,1536]{1,0:T(8,128)(2,1)S(1)}, bf16[64,1536]{1,0:T(8,128)(2,1)S(1)}, u32[]{:S(2)}, u32[]{:S(2)}) collective-permute-start(bf16[64,1536]{1,0:T(8,128)(2,1)S(1)} %fusion.47), channel_id=1, source_target_pairs={{0,64},{64,128},{128,192},{192,256},{256,320},{320,384},{384,448},... | collective-permute-start | bytes 589832 | tf_op jit(solution)/shard_map/ppermute | solution.py:12
Sparse Core Ops, SparseCore 0:
  34.7 110.9 all-gather.4
  148.9 97.9 all-gather.6
  306.3 21.6 reduce-scatter.2
  362.1 105.7 all-gather.10
  471.1 97.9 all-gather.8
  628.6 21.6 reduce-scatter.4
where the time goes:
time: 674 us; the launch traced here: 673 us
  waiting for transfers between devices  482 us (72%)
  matrix products  66.5 us (10%)
  local copies, waits for them, and re-layouts  39 us (6%)
  other arithmetic  31.6 us (5%)
  blocking collectives  27.3 us (4%)
  between operations  13.7 us (2%)
  starting transfers between devices  7.13 us (1%)
    all_gather x2, waiting for transfers between devices, per_device(): lax.all_gather(key_part, 'seq', axis=0, tiled=True)  210 us
    all_gather x2, waiting for transfers between devices, per_device(): lax.all_gather(value_part, 'seq', axis=0, tiled=True)  206 us
    reduce_scatter x2, waiting for transfers between devices, per_device(): lax.psum_scatter(jnp.einsum('hrd,hdn->rn', attended, out_heads, preferred...  43.5 us
    dot_general x8, matrix products, attend_block(): jnp.einsum('rhd,khd->hrk', query_heads, key_heads, preferred_element_type...  27.6 us
    dot_general x8, matrix products, attend_block(): jnp.einsum('hrk,khd->hrd', exponent.astype(jnp.bfloat16), value_heads, pr...  27.4 us
    all_gather x2, blocking collectives, per_device(): lax.all_gather(normed, 'head', axis=0, tiled=True)  27.3 us
    ppermute x2, waiting for transfers between devices, from_behind(): lax.ppermute(value, axis, [(i, (i + by) % length) for i in range(length)])  22 us
    dynamic_slice x32, local copies, waits for them, and re-layouts, attend_piece(): lax.scan(step_block, running, (key_stack, value_stack, jnp.arange(blocks,...  21.7 us
  transfers between devices with their start and end apart: 8, of which 8 were waited for; matrix products, arithmetic and copies ran while one was open for 0% of the time, Pallas kernels for 0%

commit v1 on v0

--- a/solution.py
+++ b/solution.py
@@ -113,12 +113,16 @@
             jnp.zeros((local_heads, query_rows), jnp.float32),
             jnp.zeros((local_heads, query_rows, HEAD), jnp.float32),
         )
+
+        def raise_rings(m):
+            local_next = jax.lax.axis_size("seq")
+            parts_out = jnp.stack([m] * local_next)
+            f_next = jax.lax.all_to_all(parts_out, axis_name="seq", split_axis=0, concat_axis=0)
+            return jnp.concatenate(f_next, axis=0)
+
         running = attend_piece(
             initial,
-            (
-                lax.all_gather(key_part, "seq", axis=0, tiled=True),
-                lax.all_gather(value_part, "seq", axis=0, tiled=True),
-            ),
+            (lax.all_gather(key_part, "seq", axis=0, tiled=True), raise_rings(value_part)),
             query_heads,
             length,
             score_scale,

time: 674 us -> 704 us (1.045)
  starting transfers between devices: 7.13 us -> 40.1 us
    all_gather x2 -> x0, waiting for transfers between devices: 206 us -> none  [per_device(): lax.all_gather(value_part, 'seq', axis=0, tiled=True)]
    all_gather x2, waiting for transfers between devices: 210 us -> 388 us  [per_device(): lax.all_gather(key_part, 'seq', axis=0, tiled=True)]
    all_to_all x0 -> x2, starting transfers between devices: none -> 32.9 us  [raise_rings(): jax.lax.all_to_all(parts_out, axis_name='seq', split_axis=0, concat_axis=0)]
    reduce_scatter x2, waiting for transfers between devices: 43.5 us -> 63.7 us  [per_device(): lax.psum_scatter(jnp.einsum('hrd,hdn->rn', attended, out_heads, preferred...]
  transfers between devices with their start and end apart: 8 -> 8, of which waited for: 8 -> 6; matrix products, arithmetic and copies ran while one was open for 0% -> 0% of each run, Pallas kernels for 0% -> 0%
where the time goes in v1:
time: 704 us; the launch traced here: 703 us
  waiting for transfers between devices  475 us (67%)
  matrix products  66.5 us (9%)
  local copies, waits for them, and re-layouts  43.1 us (6%)
  starting transfers between devices  40.1 us (6%)
  other arithmetic  31.6 us (4%)
  blocking collectives  27.4 us (4%)
  between operations  13.4 us (2%)
    all_gather x2, waiting for transfers between devices, per_device(): lax.all_gather(key_part, 'seq', axis=0, tiled=True)  388 us
    reduce_scatter x2, waiting for transfers between devices, per_device(): lax.psum_scatter(jnp.einsum('hrd,hdn->rn', attended, out_heads, preferred...  63.7 us
    all_to_all x2, starting transfers between devices, raise_rings(): jax.lax.all_to_all(parts_out, axis_name='seq', split_axis=0, concat_axis=0)  32.9 us
    dot_general x8, matrix products, attend_block(): jnp.einsum('rhd,khd->hrk', query_heads, key_heads, preferred_element_type...  27.5 us
    dot_general x8, matrix products, attend_block(): jnp.einsum('hrk,khd->hrd', exponent.astype(jnp.bfloat16), value_heads, pr...  27.4 us
    all_gather x2, blocking collectives, per_device(): lax.all_gather(normed, 'head', axis=0, tiled=True)  27.4 us
    ppermute x2, waiting for transfers between devices, from_behind(): lax.ppermute(value, axis, [(i, (i + by) % length) for i in range(length)])  22 us
    dynamic_slice x32, local copies, waits for them, and re-layouts, attend_piece(): lax.scan(step_block, running, (key_stack, value_stack, jnp.arange(blocks,...  21.7 us
  transfers between devices with their start and end apart: 8, of which 6 were waited for; matrix products, arithmetic and copies ran while one was open for 0% of the time, Pallas kernels for 0%

profile of v1, /device:TPU:8, one launch (start us, length us, event | category | flops | bytes accessed | tf_op | source)
XLA Modules:
  0.0 702.8 jit_solution(2822668099891224340)
XLA Ops:
  6.5 0.8 convert_element_type.59
  7.4 1.1 convert_reduce_fusion.1
  8.5 1.2 fusion.42
  9.6 1.1 fusion.45
  10.7 13.7 %all_gather.12 = bf16[256,1536]{1,0:T(8,128)(2,1)S(1)} all-gather(bf16[64,1536]{1,0:T(8,128)(2,1)S(1)} %fusion.45), channel_id=1, replica_groups=mesh['segment'=8,'seq'=16,'head'=4] {'head'}, dimensions={0}, use_global_device_ids=true | all-gather | bytes 983040 | tf_op jit(solution)/shard_map/all_gather | solution.py:103
  24.4 6.1 copy.30
  30.5 3.2 convolution_convert_fusion.1
  34.4 2.1 stack.4
  36.5 18.3 %all-to-all-start = ((bf16[16,256,384]{2,1,0:T(8,128)(2,1)}), bf16[16,256,384]{2,1,0:T(8,128)(2,1)}, u32[]{:S(2)}, u32[]{:S(2)}) async-start(bf16[16,256,384]{2,1,0:T(8,128)(2,1)} %stack.4), calls=%async_computation | async-start | bytes 6291456 | tf_op jit(solution)/shard_map/all_to_all | solution.py:120
  55.8 0.8 copy.33
  57.3 205.8 %all-gather.3.cloned.1.call-done = bf16[4096,384]{1,0:T(8,128)(2,1)} async-done(((bf16[256,384]{1,0:T(8,128)(2,1)}), bf16[4096,384]{1,0:T(8,128)(2,1)}) %all-gather.3.cloned.1.call-update) | async-done | bytes 3145744 | tf_op jit(solution)/shard_map/all_gather | solution.py:125
  263.1 56.5 %while.30 = (s32[]{:T(128)}, f32[3,256]{1,0:T(4,128)S(1)}, f32[3,256]{1,0:T(4,128)S(1)}, f32[3,256,128]{2,1,0:T(8,128)}, s32[4]{0:T(128)S(1)}, /*index=5*/s32[]{...) while((s32[]{:T(128)}, f32[3,256]{1,0:T(4,128)S(1)}, ...), condition=%wide.region_5.6_spmd.clone, body=%wide.region_2.5_spmd.clone.sunk | while | flops 413177600 | bytes 21483740 | solution.py:79
  264.9 1.5 constant_dynamic-slice_fusion.6
  266.7 3.4 bitcast_reduce_fusion.4
  270.2 2.5 fusion.84
  273.0 3.4 fusion.86
  276.5 0.8 copy-done.13
  279.0 1.5 constant_dynamic-slice_fusion.6
  280.8 3.4 bitcast_reduce_fusion.4
  284.3 2.5 fusion.84
  287.1 3.4 fusion.86
  290.6 0.8 copy-done.13
  293.1 1.5 constant_dynamic-slice_fusion.6
  295.0 3.4 bitcast_reduce_fusion.4
  298.4 2.5 fusion.84
  301.2 3.4 fusion.86
  304.7 0.8 copy-done.13
  307.2 1.5 constant_dynamic-slice_fusion.6
  309.1 3.4 bitcast_reduce_fusion.4
  312.5 2.5 fusion.84
  315.3 3.4 fusion.86
  319.6 2.6 fusion.30
  322.2 24.0 %reduce-scatter.3.cloned.1.call-done = bf16[64,1536]{1,0:T(8,128)(2,1)} async-done(((bf16[256,1536]{1,0:T(8,128)(2,1)}), bf16[64,1536]{1,0:T(8,128)(2,1)}) %reduce-scatter.3.cloned.1.call-update) | async-done | bytes 196624 | tf_op jit(solution)/shard_map/reduce_scatter | solution.py:132
  346.3 1.0 fusion.46
  347.3 3.5 collective-permute-start
  350.7 11.0 %collective-permute-done = bf16[64,1536]{1,0:T(8,128)(2,1)S(1)} collective-permute-done((bf16[64,1536]{1,0:T(8,128)(2,1)S(1)}, bf16[64,1536]{1,0:T(8,128)(2,1)S(1)}, u32[]{:S(2)}, u32[]{:S(2)}) %collective-permute-start) | collective-permute-done | bytes 196640 | tf_op jit(solution)/shard_map/ppermute | solution.py:12
  362.6 13.7 %all_gather.14 = bf16[256,1536]{1,0:T(8,128)(2,1)S(1)} all-gather(bf16[64,1536]{1,0:T(8,128)(2,1)S(1)} %fusion.41), channel_id=1, replica_groups=mesh['segment'=8,'seq'=16,'head'=4] {'head'}, dimensions={0}, use_global_device_ids=true | all-gather | bytes 983040 | tf_op jit(solution)/shard_map/all_gather | solution.py:103
  376.2 3.2 convolution_convert_fusion
  380.2 2.1 stack.5
  382.3 14.5 %all-to-all-start.1 = ((bf16[16,256,384]{2,1,0:T(8,128)(2,1)}), bf16[16,256,384]{2,1,0:T(8,128)(2,1)}, u32[]{:S(2)}, u32[]{:S(2)}) async-start(bf16[16,256,384]{2,1,0:T(8,128)(2,1)} %stack.5), calls=%async_computation.2 | async-start | bytes 6291456 | tf_op jit(solution)/shard_map/all_to_all | solution.py:120
  398.0 0.8 copy.37
  398.8 182.4 %all-gather.5.cloned.1.call-done = bf16[4096,384]{1,0:T(8,128)(2,1)} async-done(((bf16[256,384]{1,0:T(8,128)(2,1)}), bf16[4096,384]{1,0:T(8,128)(2,1)}) %all-gather.5.cloned.1.call-update) | async-done | bytes 3145744 | tf_op jit(solution)/shard_map/all_gather | solution.py:125
  581.2 56.7 %while.31 = (s32[]{:T(128)}, f32[3,256]{1,0:T(4,128)S(1)}, f32[3,256]{1,0:T(4,128)S(1)}, f32[3,256,128]{2,1,0:T(8,128)}, s32[4]{0:T(128)S(1)}, /*index=5*/s32[]{...) while((s32[]{:T(128)}, f32[3,256]{1,0:T(4,128)S(1)}, ...), condition=%wide.region_12.13_spmd.clone, body=%wide.region_9.12_spmd.clone.sunk | while | flops 413177600 | bytes 21483740 | solution.py:79
  583.1 1.5 constant_dynamic-slice_fusion.7
  584.9 3.4 bitcast_reduce_fusion.5
  588.4 2.5 fusion.91
  591.2 3.4 fusion.93
  597.3 1.5 constant_dynamic-slice_fusion.7
  599.1 3.4 bitcast_reduce_fusion.5
  602.6 2.5 fusion.91
  605.4 3.4 fusion.93
  611.5 1.5 constant_dynamic-slice_fusion.7
  613.3 3.4 bitcast_reduce_fusion.5
  616.8 2.5 fusion.91
  619.6 3.4 fusion.93
  625.6 1.5 constant_dynamic-slice_fusion.7
  627.5 3.4 bitcast_reduce_fusion.5
  630.9 2.5 fusion.91
  633.8 3.4 fusion.93
  637.9 2.6 fusion.31
  640.5 39.6 %reduce-scatter.5.cloned.1.call-done = bf16[64,1536]{1,0:T(8,128)(2,1)} async-done(((bf16[256,1536]{1,0:T(8,128)(2,1)}), bf16[64,1536]{1,0:T(8,128)(2,1)}) %reduce-scatter.5.cloned.1.call-update) | async-done | bytes 196624 | tf_op jit(solution)/shard_map/reduce_scatter | solution.py:132
  680.2 1.0 fusion.47
  681.2 3.5 collective-permute-start.1
  684.6 11.0 %collective-permute-done.1 = bf16[64,1536]{1,0:T(8,128)(2,1)S(1)} collective-permute-done((bf16[64,1536]{1,0:T(8,128)(2,1)S(1)}, bf16[64,1536]{1,0:T(8,128)(2,1)S(1)}, u32[]{:S(2)}, u32[]{:S(2)}) %collective-permute-start.1) | collective-permute-done | bytes 196640 | tf_op jit(solution)/shard_map/ppermute | solution.py:12
  (142 shorter events, 23.9 us)
Async XLA Ops:
  6.5 313.0 %copy-start = (bf16[1,384,1536]{2,1,0:T(8,128)(2,1)S(1)}, bf16[1,384,1536]{2,1,0:T(8,128)(2,1)}, u32[]{:S(2)}) copy-start(bf16[1,384,1536]{2,1,0:T(8,128)(2,1)} %param.15) | copy-start | bytes 3538948
  7.4 2.3 copy-start.6
  7.4 3.3 copy-start.8
  36.5 20.1 %copy-start.11 = (s32[8]{0:T(128)S(1)}, s32[8]{0:T(128)}, u32[]{:S(2)}) copy-start(s32[8]{0:T(128)} %param.11) | copy-start | bytes 100
  36.5 226.6 %all-to-all-start = ((bf16[16,256,384]{2,1,0:T(8,128)(2,1)}), bf16[16,256,384]{2,1,0:T(8,128)(2,1)}, u32[]{:S(2)}, u32[]{:S(2)}) async-start(bf16[16,256,384]{2,1,0:T(8,128)(2,1)} %stack.4), calls=%async_computation | async-start | bytes 6291456 | tf_op jit(solution)/shard_map/all_to_all | solution.py:120
  54.8 208.3 %all-gather.3.cloned.1.call-start = ((), (), s32[]{:S(2)}) async-start(), calls=%async_computation.4 | async-start | bytes 3342336 | tf_op jit(solution)/shard_map/all_gather | solution.py:125
  55.5 290.7 %reduce-scatter.3.cloned.1.call-start = ((), (), s32[]{:S(2)}) async-start(), calls=%async_computation.5 | async-start | bytes 983040 | tf_op jit(solution)/shard_map/reduce_scatter | solution.py:132
  270.2 2.8 copy-start.12
  276.4 0.8 copy-start.13
  284.3 2.8 copy-start.12
  290.5 0.8 copy-start.13
  298.4 2.8 copy-start.12
  304.7 0.8 copy-start.13
  312.5 2.8 copy-start.12
  318.8 0.8 copy-start.13
  319.6 2.6 copy-start.10
  319.6 26.7 %copy-start.1 = (bf16[1,64,1536]{2,1,0:T(8,128)(2,1)S(1)}, bf16[1,64,1536]{2,1,0:T(8,128)(2,1)}, u32[]{:S(2)}) copy-start(bf16[1,64,1536]{2,1,0:T(8,128)(2,1)} %param.10) | copy-start | bytes 589828
  319.6 42.8 %copy-start.7 = (f32[1536]{0:T(1024)S(1)}, f32[1536]{0:T(1024)}, u32[]{:S(2)}) copy-start(f32[1536]{0:T(1024)} %copy-done.6) | copy-start | bytes 18436
  319.6 42.8 %copy-start.9 = (f32[1536]{0:T(1024)S(1)}, f32[1536]{0:T(1024)}, u32[]{:S(2)}) copy-start(f32[1536]{0:T(1024)} %copy-done.8) | copy-start | bytes 18436
  322.2 57.3 %copy-start.4 = (f32[1536]{0:T(1024)}, f32[1536]{0:T(1024)S(1)}, u32[]{:S(2)}) copy-start(f32[1536]{0:T(1024)S(1)} %convert_reduce_fusion.2) | copy-start | bytes 18436
  347.3 14.5 %collective-permute-start = (bf16[64,1536]{1,0:T(8,128)(2,1)S(1)}, bf16[64,1536]{1,0:T(8,128)(2,1)S(1)}, u32[]{:S(2)}, u32[]{:S(2)}) collective-permute-start(bf16[64,1536]{1,0:T(8,128)(2,1)S(1)} %fusion.46), channel_id=1, source_target_pairs={{0,64},{64,128},{128,192},{192,256},{256,320},{320,384},{384,448},... | collective-permute-start | bytes 589832 | tf_op jit(solution)/shard_map/ppermute | solution.py:12
  361.7 0.7 copy-start.2
  382.3 198.9 %all-to-all-start.1 = ((bf16[16,256,384]{2,1,0:T(8,128)(2,1)}), bf16[16,256,384]{2,1,0:T(8,128)(2,1)}, u32[]{:S(2)}, u32[]{:S(2)}) async-start(bf16[16,256,384]{2,1,0:T(8,128)(2,1)} %stack.5), calls=%async_computation.2 | async-start | bytes 6291456 | tf_op jit(solution)/shard_map/all_to_all | solution.py:120
  396.9 184.3 %all-gather.5.cloned.1.call-start = ((), (), s32[]{:S(2)}) async-start(), calls=%async_computation.6 | async-start | bytes 3342336 | tf_op jit(solution)/shard_map/all_gather | solution.py:125
  397.6 282.5 %reduce-scatter.5.cloned.1.call-start = ((), (), s32[]{:S(2)}) async-start(), calls=%async_computation.7 | async-start | bytes 983040 | tf_op jit(solution)/shard_map/reduce_scatter | solution.py:132
  588.4 2.8 copy-start.14
  594.7 0.8 copy-start.15
  602.6 2.8 copy-start.14
  608.8 0.8 copy-start.15
  616.7 2.8 copy-start.14
  623.0 0.8 copy-start.15
  630.9 2.8 copy-start.14
  637.2 0.8 copy-start.15
  637.9 42.2 %copy-start.3 = (bf16[64,1536]{1,0:T(8,128)(2,1)S(1)}, bf16[64,1536]{1,0:T(8,128)(2,1)}, u32[]{:S(2)}) copy-start(bf16[64,1536]{1,0:T(8,128)(2,1)} %copy-done.2) | copy-start | bytes 589828
  637.9 42.2 %copy-start.5 = (f32[1536]{0:T(1024)S(1)}, f32[1536]{0:T(1024)}, u32[]{:S(2)}) copy-start(f32[1536]{0:T(1024)} %copy-done.4) | copy-start | bytes 18436
  681.2 14.5 %collective-permute-start.1 = (bf16[64,1536]{1,0:T(8,128)(2,1)S(1)}, bf16[64,1536]{1,0:T(8,128)(2,1)S(1)}, u32[]{:S(2)}, u32[]{:S(2)}) collective-permute-start(bf16[64,1536]{1,0:T(8,128)(2,1)S(1)} %fusion.47), channel_id=1, source_target_pairs={{0,64},{64,128},{128,192},{192,256},{256,320},{320,384},{384,448},... | collective-permute-start | bytes 589832 | tf_op jit(solution)/shard_map/ppermute | solution.py:12
Sparse Core Ops, SparseCore 0:
  59.0 204.0 all-gather.2
  322.3 23.9 reduce-scatter.2
  401.0 180.1 all-gather.4
  640.6 39.4 reduce-scatter.4
